TPU v7x, 32 devices: a whole 2x2x4 slice. The times are simulated.
32 devices in a mesh: wave: 16 (over z, x, core), level: 2 (over y).
Axes of the slice: x: 2, y: 2, z: 4, core: 2. Of those that a mesh axis runs over, the one named last changes fastest.
Arguments:
- state: float32 [4, 64, 256, 2, 256], P(None, 'level', 'wave'), may hold values from -0.02 to 0.02
- legendre: float32 [256, 384, 256], P('wave'), may hold values from -6 to 6
- lat_weight: float32 [384], P('wave'), may hold values from 0.8 to 2
- modes: float32 [64, 64], replicated, may hold values from -1 to 1, as said below
- mode_rates: float32 [64], replicated, may hold values from 1e-05 to 0.003
- diffusion: float32 [4], replicated, may hold values from 0.3 to 3
- norm_gain: float32 [256], replicated, may hold values from 0.5 to 1.5
- w_first: bfloat16 [1024, 256], replicated, may hold values from -0.375 to 0.375
- b_first: float32 [1024], replicated, may hold values from -3 to 3
- w_second: bfloat16 [1024, 1024], replicated, may hold values from -0.1875 to 0.1875
- b_second: float32 [1024], replicated, may hold values from -3 to 3
- w_third: bfloat16 [256, 1024], replicated, may hold values from -0.1875 to 0.1875
- b_third: float32 [256], replicated, may hold values from -1.2 to 1.2
Outputs:
- next_state: float32 [4, 64, 256, 2, 256], P(None, 'level', 'wave')
Inputs may be any that keep to these rules, and one draw needn't show every extreme that they name: `modes`: orthogonal: its transpose is its inverse.
All inputs are finite; a program needn't handle non-finite values.
Results may differ from a plain program's by a relative error of at most 0.0011.
Values may be sent and summed in bfloat16 or wider, within the bound.
A program may use at most 192 MiB of HBM per device.

v0:
```python
import jax
import jax.numpy as jnp
from jax import lax
from jax.sharding import PartitionSpec as P

M = 256
LAT = 384
LON = 768
highest = lax.Precision.HIGHEST
norm_eps = 1e-06


def phase_angles(waves, longitudes):
    wave_idx = jnp.arange(waves, dtype=jnp.int32)
    lon_idx = jnp.arange(longitudes, dtype=jnp.int32)
    phase_turns = wave_idx[:, None] * lon_idx[None, :] % longitudes
    return (2.0 * jnp.pi / longitudes * phase_turns.astype(jnp.float32), wave_idx)


def synthesis_table(waves, longitudes):
    angle_table, wave_idx = phase_angles(waves, longitudes)
    factor = jnp.where(wave_idx == 0, 1.0, 2.0).astype(jnp.float32)[:, None]
    return jnp.stack([factor * jnp.cos(angle_table), -factor * jnp.sin(angle_table)], axis=1)


def analysis_table(waves, longitudes):
    angle_table, wave_idx = phase_angles(waves, longitudes)
    flipped = angle_table.T
    return jnp.stack([jnp.cos(flipped), -jnp.sin(flipped)], axis=2) / longitudes


def column_physics(columns, norm_gain, w_first, b_first, w_second, b_second, w_third, b_third):
    values = columns.astype(jnp.float32)
    inverse_rms = lax.rsqrt(jnp.mean(values * values, axis=0, keepdims=True) + norm_eps)
    normed = (values * inverse_rms * norm_gain[:, None]).astype(jnp.bfloat16)
    hidden_one = jax.nn.gelu(
        jnp.dot(w_first, normed, preferred_element_type=jnp.float32) + b_first[:, None]
    ).astype(jnp.bfloat16)
    hidden_two = jax.nn.gelu(
        jnp.dot(w_second, hidden_one, preferred_element_type=jnp.float32) + b_second[:, None]
    ).astype(jnp.bfloat16)
    return (
        jnp.dot(w_third, hidden_two, preferred_element_type=jnp.float32) + b_third[:, None]
    ).astype(jnp.bfloat16)


def body(
    state,
    legendre,
    lat_weight,
    modes,
    mode_rates,
    diffusion,
    norm_gain,
    w_first,
    b_first,
    w_second,
    b_second,
    w_third,
    b_third,
):
    fields = state.shape[0]
    lev_dev = state.shape[1]
    m_dev = state.shape[2]
    complex_parts = state.shape[3]
    degrees = state.shape[4]
    levels = modes.shape[0]
    wave_count = lax.axis_size("wave")
    lat_dev = LAT // wave_count
    wave_global = lax.axis_index("wave") * m_dev + jnp.arange(m_dev, dtype=jnp.int32)
    degree_index = wave_global[:, None] + jnp.arange(degrees, dtype=jnp.int32)[None, :]
    kept_mask = (degree_index < M).astype(jnp.float32)
    kept_basis = legendre * kept_mask[:, None, :]
    basis_blocks = kept_basis.reshape(m_dev, wave_count, lat_dev, degrees)
    inverse_tab = synthesis_table(M, LON).reshape(wave_count, m_dev, complex_parts, LON)
    forward_tab = analysis_table(M, LON).reshape(LON, wave_count, m_dev, complex_parts)
    pieces = []
    for field_index in range(fields):
        band_coeffs = jnp.einsum(
            "lmcj,mwaj->wlcma", state[field_index], basis_blocks, precision=highest
        )
        exchanged = lax.all_to_all(
            band_coeffs.reshape(wave_count, -1), "wave", split_axis=0, concat_axis=0, tiled=True
        )
        shaped = exchanged.reshape(wave_count, lev_dev, complex_parts, m_dev, lat_dev)
        pieces.append(jnp.einsum("wlcma,wmco->lao", shaped, inverse_tab, precision=highest))
    grid_field = jnp.stack(pieces)
    grid_low = grid_field.astype(jnp.bfloat16)
    slab = grid_low.reshape(fields, lev_dev, lat_dev * LON)
    columns = lax.all_to_all(slab, "level", split_axis=2, concat_axis=1, tiled=True)
    col_count = columns.shape[2]
    tendency = column_physics(
        columns.reshape(fields * levels, col_count),
        norm_gain,
        w_first,
        b_first,
        w_second,
        b_second,
        w_third,
        b_third,
    )
    tendency = tendency.reshape(fields, levels, col_count)
    returned = lax.all_to_all(tendency, "level", split_axis=1, concat_axis=2, tiled=True).reshape(
        fields, lev_dev, lat_dev, LON
    )
    updated = (grid_field + returned.astype(jnp.float32)) * lat_weight[None, None, :, None]
    field_parts = []
    for field_index in range(fields):
        wave_coeffs = jnp.einsum(
            "lao,owmc->wlcma", updated[field_index], forward_tab, precision=highest
        )
        exchanged = lax.all_to_all(
            wave_coeffs.reshape(wave_count, -1), "wave", split_axis=0, concat_axis=0, tiled=True
        )
        shaped = exchanged.reshape(wave_count, lev_dev, complex_parts, m_dev, lat_dev)
        field_parts.append(jnp.einsum("wlcma,mwaj->lmcj", shaped, basis_blocks, precision=highest))
    spectral = jnp.stack(field_parts)
    growth = (degree_index * (degree_index + 1)).astype(jnp.float32)
    divisor = 1.0 + mode_rates[:, None, None, None] * growth[None, :, None, :]
    divisor = jnp.broadcast_to(divisor, (levels, m_dev, complex_parts, degrees)).reshape(levels, -1)
    divergence = spectral[1].reshape(lev_dev, -1)
    lev_start = lax.axis_index("level") * lev_dev
    own_rows = lax.dynamic_slice_in_dim(modes, lev_start, lev_dev, 0)
    amplitude = jnp.dot(
        modes.T,
        lax.all_gather(divergence, "level", axis=0, tiled=True),
        precision=highest,
        preferred_element_type=jnp.float32,
    )
    amplitude = amplitude / divisor
    solved = jnp.dot(own_rows, amplitude, precision=highest, preferred_element_type=jnp.float32)
    solved = solved.reshape(lev_dev, m_dev, complex_parts, degrees)
    combined = jnp.concatenate([spectral[:1], solved[None], spectral[2:]], axis=0)
    scaled_growth = growth / (M * (M - 1))
    damping = 1.0 + diffusion[:, None, None] * (scaled_growth * scaled_growth)[None]
    return combined / damping[:, None, :, None, :]


def solution(mesh):
    in_specs = (
        P(None, "level", "wave", None, None),
        P("wave", None, None),
        P("wave"),
        P(),
        P(),
        P(),
        P(),
        P(),
        P(),
        P(),
        P(),
        P(),
        P(),
    )
    out_specs = P(None, "level", "wave", None, None)
    return jax.shard_map(body, mesh=mesh, in_specs=in_specs, out_specs=out_specs, check_vma=False)
```

profile of v0, /device:TPU:0, one launch (start us, length us, event | category | flops | bytes accessed | tf_op | source)
XLA Modules:
  0.0 1027.8 jit_solution(9725989835272598431)
XLA Ops:
  133.4 12.3 %convolution_bitcast_fusion.5 = f32[16,32,2,16,24]{1,4,2,0,3:T(8,128)} fusion(f32[16,16,24,256,1]{3,2,4,1,0:T(8,128)} %bitcast.214, f32[1,32,16,2,256]{4,3,2,1,0:T(2,128)S(1)} %get-tuple-element.12), kind=kOutput, calls=%fused_computation.49 | convolution fusion | flops 1207959552 | bytes 8912896 | tf_op jit(solution)/shard_map/lmcj,mwaj->wlcma/dot_general | solution.py:79
  194.9 18.3 %bitcast_convert_fusion.3 = (bf16[32,24,768]{2,1,0:T(8,128)(2,1)}, f32[32,24,768,1,1]{2,1,3,0,4:T(8,128)}) fusion(f32[16,32,2,16,24]{4,3,2,1,0:T(8,128)} %reshape.350, f32[16,16,1,768]{3,1,2,0:T(8,128)} %get-tuple-element.16, f32[16,16,1,768]{3,1,2,0:T(8,128)S(1)} %get-tuple-element.15), kind=kOutput, calls=%fused_computation.64 | convolution fusion | flops 3624861696 | bytes 6684672 | tf_op jit(solution)/shard_map/wlcma,wmco->lao/dot_general | solution.py:86
  231.4 17.9 %bitcast_convert_fusion.2 = (bf16[32,24,768]{2,1,0:T(8,128)(2,1)}, f32[32,24,768,1,1]{2,1,3,0,4:T(8,128)}) fusion(f32[16,32,2,16,24]{4,3,2,1,0:T(8,128)} %reshape.351, f32[16,16,1,768]{3,1,2,0:T(8,128)} %get-tuple-element.16, f32[16,16,1,768]{3,1,2,0:T(8,128)S(1)} %get-tuple-element.15), kind=kOutput, calls=%fused_computation.63 | convolution fusion | flops 3624861696 | bytes 6684672 | tf_op jit(solution)/shard_map/wlcma,wmco->lao/dot_general | solution.py:86
  267.5 17.8 %bitcast_convert_fusion.1 = (bf16[32,24,768]{2,1,0:T(8,128)(2,1)}, f32[32,24,768,1,1]{2,1,3,0,4:T(8,128)}) fusion(f32[16,32,2,16,24]{4,3,2,1,0:T(8,128)} %reshape.352, f32[16,16,1,768]{3,1,2,0:T(8,128)} %get-tuple-element.16, f32[16,16,1,768]{3,1,2,0:T(8,128)S(1)} %get-tuple-element.15), kind=kOutput, calls=%fused_computation.62 | convolution fusion | flops 3624861696 | bytes 6684672 | tf_op jit(solution)/shard_map/wlcma,wmco->lao/dot_general | solution.py:86
  303.7 17.8 %bitcast_convert_fusion = (bf16[32,24,768]{2,1,0:T(8,128)(2,1)}, f32[32,24,768,1,1]{2,1,3,0,4:T(8,128)}) fusion(f32[16,32,2,16,24]{4,3,2,1,0:T(8,128)} %reshape.353, f32[16,16,1,768]{3,1,2,0:T(8,128)} %get-tuple-element.16, f32[16,16,1,768]{3,1,2,0:T(8,128)S(1)} %get-tuple-element.15), kind=kOutput, calls=%fused_computation.61 | convolution fusion | flops 3624861696 | bytes 6684672 | tf_op jit(solution)/shard_map/wlcma,wmco->lao/dot_general | solution.py:86
  327.0 22.5 %copy.204 = bf16[4,32,18432]{1,0,2:T(4,128)(2,1)} copy(bf16[4,32,18432]{2,1,0:T(8,128)(2,1)} %pad_maximum_fusion) | data formatting | bytes 9437184 | tf_op jit(solution)/shard_map/stack | solution.py:87
  349.5 27.9 %reshape.391 = bf16[2,2,589824]{2,1,0:T(2,128)(2,1)} reshape(bf16[18432,4,32]{2,1,0:T(4,128)(2,1)} %bitcast.221) | data formatting | bytes 9437184
  377.5 61.9 %all_to_all.98 = bf16[2,2,589824]{2,1,0:T(2,128)(2,1)} all-to-all(bf16[2,2,589824]{2,1,0:T(2,128)(2,1)} %reshape.391), channel_id=1, replica_groups=mesh['wave'=16,'level'=2] {'level'}, dimensions={0} | all-to-all | bytes 9437184 | tf_op jit(solution)/shard_map/all_to_all | solution.py:90
  439.4 20.3 %reshape.392 = bf16[18432,4,32]{2,1,0:T(4,128)(2,1)} reshape(bf16[2,2,589824]{2,1,0:T(2,128)(2,1)} %all_to_all.98) | data formatting | bytes 9437184
  459.7 22.8 %copy.205 = bf16[4,32,18432]{2,1,0:T(8,128)(2,1)} copy(bf16[4,32,18432]{1,0,2:T(4,128)(2,1)} %bitcast.222) | data formatting | bytes 9437184 | tf_op jit(solution)/shard_map/all_to_all | solution.py:90
  482.5 12.7 %reshape.362 = f32[4,32,2,9216]{3,2,1,0:T(2,128)} reshape(bf16[4,32,18432]{2,1,0:T(8,128)(2,1)} %copy.205) | data formatting | bytes 14155776 | tf_op jit(solution)/shard_map/convert_element_type | solution.py:33
  513.9 19.4 %fusion.7.clone.4 = bf16[1024,9216]{0,1:T(8,128)(2,1)} fusion(bf16[256,9216]{1,0:T(8,128)(2,1)S(1)} %fusion.24, bf16[1024,256]{1,0:T(8,128)(2,1)S(1)} %copy-done.17, f32[1024]{0:T(1024)S(1)} %copy-done.19), kind=kOutput, calls=%fused_computation.9.clone.clone.clone.1 | convolution fusion | flops 4926210048 | bytes 24121344 | tf_op jit(solution)/shard_map/dot_general | solution.py:37
  533.4 38.6 %fusion.15 = bf16[1024,9216]{0,1:T(8,128)(2,1)} fusion(bf16[1024,1024]{1,0:T(8,128)(2,1)S(1)} %copy-done, f32[1024]{0:T(1024)S(1)} %copy-done.20, bf16[1024,9216]{0,1:T(8,128)(2,1)} %fusion.7.clone.4), kind=kOutput, calls=%fused_computation.17 | convolution fusion | flops 19421724672 | bytes 39849984 | tf_op jit(solution)/shard_map/dot_general | solution.py:40
  571.9 19.2 %fusion.21 = bf16[9216,256]{0,1:T(8,128)(2,1)S(1)} fusion(bf16[1024,9216]{0,1:T(8,128)(2,1)} %fusion.15, bf16[256,1024]{1,0:T(8,128)(2,1)S(1)} %copy-done.18, f32[256]{0:T(256)S(1)} %copy-done.21), kind=kOutput, calls=%fused_computation.24 | convolution fusion | flops 4836556800 | bytes 24118272 | tf_op jit(solution)/shard_map/dot_general | solution.py:43
  606.2 49.7 %all-to-all-done.5 = bf16[4,64,9216]{2,0,1:T(4,128)(2,1)} async-done(((bf16[4,64,9216]{2,0,1:T(4,128)(2,1)}), bf16[4,64,9216]{2,0,1:T(4,128)(2,1)}, u32[]{:S(2)}, u32[]{:S(2)}) %all-to-all-start.5) | async-done | bytes 4718624 | tf_op jit(solution)/shard_map/all_to_all | solution.py:103
  669.1 13.1 %reshape.361 = f32[4,32,24,768]{3,2,1,0:T(8,128)} reshape(f32[4,32,2,9216]{3,2,1,0:T(2,128)} %copy.209) | data formatting | bytes 18874368 | tf_op jit(solution)/shard_map/convert_element_type | solution.py:106
  692.5 17.0 %convolution_bitcast_fusion.3 = f32[16,32,2,16,24]{1,3,4,2,0:T(8,128)} fusion(f32[32,24,768,1,1]{2,1,0,4,3:T(8,128)S(1)} %get-tuple-element.8, f32[768,16,16,1]{0,2,3,1:T(8,128)S(1)} %get-tuple-element.14, f32[768,16,16,1]{0,2,3,1:T(8,128)S(1)} %get-tuple-element.13), kind=kOutput, calls=%fused_computation.47 | convolution fusion | flops 3624665088 | bytes 5505024 | tf_op jit(solution)/shard_map/lao,owmc->wlcma/dot_general | solution.py:109
  734.7 18.4 %convolution_bitcast_fusion.4 = f32[16,32,2,16,24]{1,3,4,2,0:T(8,128)} fusion(f32[32,24,768,1,1]{2,1,0,4,3:T(8,128)} %get-tuple-element.5, f32[768,16,16,1]{0,2,3,1:T(8,128)} %copy-done.7, f32[768,16,16,1]{0,2,3,1:T(8,128)S(1)} %get-tuple-element.13), kind=kOutput, calls=%fused_computation.48 | convolution fusion | flops 3624665088 | bytes 5505024 | tf_op jit(solution)/shard_map/lao,owmc->wlcma/dot_general | solution.py:109
  780.1 18.4 %convolution_bitcast_fusion.2 = f32[16,32,2,16,24]{1,3,4,2,0:T(8,128)} fusion(f32[32,24,768,1,1]{2,1,0,4,3:T(8,128)} %get-tuple-element.7, f32[768,16,16,1]{0,2,3,1:T(8,128)} %copy-done.7, f32[768,16,16,1]{0,2,3,1:T(8,128)S(1)} %get-tuple-element.13), kind=kOutput, calls=%fused_computation.46 | convolution fusion | flops 3624665088 | bytes 5505024 | tf_op jit(solution)/shard_map/lao,owmc->wlcma/dot_general | solution.py:109
  824.8 18.4 %convolution_bitcast_fusion.1 = f32[16,32,2,16,24]{1,3,4,2,0:T(8,128)} fusion(f32[32,24,768,1,1]{2,1,0,4,3:T(8,128)} %get-tuple-element.6, f32[768,16,16,1]{0,2,3,1:T(8,128)} %copy-done.7, f32[768,16,16,1]{0,2,3,1:T(8,128)S(1)} %get-tuple-element.13), kind=kOutput, calls=%fused_computation.45 | convolution fusion | flops 3624665088 | bytes 5505024 | tf_op jit(solution)/shard_map/lao,owmc->wlcma/dot_general | solution.py:109
  882.9 18.7 %fusion.42 = f32[32,16,2,256]{3,0,2,1:T(8,128)S(1)} fusion(f32[16,16,24,256,1]{3,2,1,4,0:T(8,128)} %bitcast.215, f32[16,32,2,16,24]{4,3,2,1,0:T(8,128)} %reshape.356), kind=kOutput, calls=%fused_computation.69 | convolution fusion | flops 1207959552 | bytes 8912896 | tf_op jit(solution)/shard_map/wlcma,mwaj->lmcj/dot_general | solution.py:116
  948.3 18.6 %fusion.39 = f32[1,32,16,2,256]{4,1,3,2,0:T(8,128)S(1)} fusion(f32[16,16,24,256,1]{3,2,1,4,0:T(8,128)} %bitcast.216, f32[16,32,2,16,24]{4,3,2,1,0:T(8,128)} %reshape.355), kind=kOutput, calls=%fused_computation.68 | convolution fusion | flops 1207959552 | bytes 8912896 | tf_op jit(solution)/shard_map/wlcma,mwaj->lmcj/dot_general | solution.py:116
  966.9 20.0 %fusion.45 = f32[1,32,16,2,256]{4,1,3,2,0:T(8,128)} fusion(f32[16,16,24,256,1]{3,2,1,4,0:T(8,128)} %bitcast.217, f32[16,32,2,16,24]{4,3,2,1,0:T(8,128)} %reshape.358), kind=kOutput, calls=%fused_computation.70 | convolution fusion | flops 1207959552 | bytes 8912896 | tf_op jit(solution)/shard_map/wlcma,mwaj->lmcj/dot_general | solution.py:116
  987.0 19.6 %fusion.48 = f32[1,32,16,2,256]{4,1,3,2,0:T(8,128)} fusion(f32[16,16,24,256,1]{3,2,1,4,0:T(8,128)S(1)} %bitcast.220, f32[16,32,2,16,24]{4,3,2,1,0:T(8,128)S(1)} %bitcast.224), kind=kOutput, calls=%fused_computation.71 | convolution fusion | flops 1207959552 | bytes 8912896 | tf_op jit(solution)/shard_map/wlcma,mwaj->lmcj/dot_general | solution.py:116
  (148 shorter events, 472.1 us)
Async XLA Ops:
  6.5 526.8 %copy-start = (bf16[1024,1024]{1,0:T(8,128)(2,1)S(1)}, bf16[1024,1024]{1,0:T(8,128)(2,1)}, u32[]{:S(2)}) copy-start(bf16[1024,1024]{1,0:T(8,128)(2,1)} %param.22) | copy-start | bytes 6291460
  43.7 39.5 %all-to-all-start = ((f32[16,1,24576]{2,1,0:T(1,128)}), f32[16,1,24576]{2,1,0:T(1,128)}, u32[]{:S(2)}, u32[]{:S(2)}) async-start(f32[16,1,24576]{2,1,0:T(1,128)} %all_to_all.80), calls=%async_computation | async-start | bytes 3145728 | tf_op jit(solution)/shard_map/all_to_all | solution.py:82
  83.2 41.0 %all-to-all-start.1 = ((f32[16,1,24576]{2,1,0:T(1,128)}), f32[16,1,24576]{2,1,0:T(1,128)}, u32[]{:S(2)}, u32[]{:S(2)}) async-start(f32[16,1,24576]{2,1,0:T(1,128)} %all_to_all.81), calls=%async_computation.1 | async-start | bytes 3145728 | tf_op jit(solution)/shard_map/all_to_all | solution.py:82
  124.2 41.1 %all-to-all-start.2 = ((f32[16,1,24576]{2,1,0:T(1,128)}), f32[16,1,24576]{2,1,0:T(1,128)}, u32[]{:S(2)}, u32[]{:S(2)}) async-start(f32[16,1,24576]{2,1,0:T(1,128)} %all_to_all.82), calls=%async_computation.2 | async-start | bytes 3145728 | tf_op jit(solution)/shard_map/all_to_all | solution.py:82
  165.3 122.8 %all-to-all-start.3 = ((f32[16,1,24576]{2,1,0:T(1,128)}), f32[16,1,24576]{2,1,0:T(1,128)}, u32[]{:S(2)}, u32[]{:S(2)}) async-start(f32[16,1,24576]{2,1,0:T(1,128)} %all_to_all.83), calls=%async_computation.3 | async-start | bytes 3145728 | tf_op jit(solution)/shard_map/all_to_all | solution.py:82
  513.9 19.4 %copy-start.20 = (f32[1024]{0:T(1024)S(1)}, f32[1024]{0:T(1024)}, u32[]{:S(2)}) copy-start(f32[1024]{0:T(1024)} %param.23) | copy-start | bytes 12292
  533.4 38.6 %copy-start.18 = (bf16[256,1024]{1,0:T(8,128)(2,1)S(1)}, bf16[256,1024]{1,0:T(8,128)(2,1)}, u32[]{:S(2)}) copy-start(bf16[256,1024]{1,0:T(8,128)(2,1)} %param.24) | copy-start | bytes 1572868
  533.4 38.6 %copy-start.21 = (f32[256]{0:T(256)S(1)}, f32[256]{0:T(256)}, u32[]{:S(2)}) copy-start(f32[256]{0:T(256)} %param.25) | copy-start | bytes 3076
  597.0 58.9 %all-to-all-start.5 = ((bf16[4,64,9216]{2,0,1:T(4,128)(2,1)}), bf16[4,64,9216]{2,0,1:T(4,128)(2,1)}, u32[]{:S(2)}, u32[]{:S(2)}) async-start(bf16[4,64,9216]{2,0,1:T(4,128)(2,1)} %copy.207), calls=%async_computation.5 | async-start | bytes 9437184 | tf_op jit(solution)/shard_map/all_to_all | solution.py:103
  606.2 86.3 %copy-start.7 = (f32[768,16,16,1]{0,2,3,1:T(8,128)}, f32[768,16,16,1]{0,2,3,1:T(8,128)S(1)}, u32[]{:S(2)}) copy-start(f32[768,16,16,1]{0,2,3,1:T(8,128)S(1)} %get-tuple-element.14) | copy-start | bytes 2359300
  729.2 43.5 %all-to-all-start.7 = ((f32[16,1,24576]{2,1,0:T(1,128)}), f32[16,1,24576]{2,1,0:T(1,128)S(1)}, u32[]{:S(2)}, u32[]{:S(2)}) async-start(f32[16,1,24576]{2,1,0:T(1,128)} %all_to_all.85), calls=%async_computation.7 | async-start | bytes 3145728 | tf_op jit(solution)/shard_map/all_to_all | solution.py:112
  773.9 44.3 %all-to-all-start.6 = ((f32[16,1,24576]{2,1,0:T(1,128)}), f32[16,1,24576]{2,1,0:T(1,128)S(1)}, u32[]{:S(2)}, u32[]{:S(2)}) async-start(f32[16,1,24576]{2,1,0:T(1,128)} %all_to_all.84), calls=%async_computation.6 | async-start | bytes 3145728 | tf_op jit(solution)/shard_map/all_to_all | solution.py:112
  818.2 25.0 %copy-start.4 = (f32[16,1,24576]{2,1,0:T(1,128)}, f32[16,1,24576]{2,1,0:T(1,128)S(1)}, u32[]{:S(2)}) copy-start(f32[16,1,24576]{2,1,0:T(1,128)S(1)} %all-to-all-done.6) | copy-start | bytes 4718596
  818.2 44.7 %all-to-all-start.8 = ((f32[16,1,24576]{2,1,0:T(1,128)}), f32[16,1,24576]{2,1,0:T(1,128)}, u32[]{:S(2)}, u32[]{:S(2)}) async-start(f32[16,1,24576]{2,1,0:T(1,128)} %all_to_all.86), calls=%async_computation.8 | async-start | bytes 3145728 | tf_op jit(solution)/shard_map/all_to_all | solution.py:112
  853.7 15.4 %copy-start.12 = (s32[16]{0:T(128)S(1)}, s32[16]{0:T(128)}, u32[]{:S(2)}) copy-start(s32[16]{0:T(128)} %copy-done.11) | copy-start | bytes 196
  853.7 15.5 %copy-start.14 = (f32[64]{0:T(128)S(1)}, f32[64]{0:T(128)}, u32[]{:S(2)}) copy-start(f32[64]{0:T(128)} %param.17) | copy-start | bytes 772
  862.9 71.9 %all-to-all-start.9 = ((f32[16,1,24576]{2,1,0:T(1,128)}), f32[16,1,24576]{2,1,0:T(1,128)}, u32[]{:S(2)}, u32[]{:S(2)}) async-start(f32[16,1,24576]{2,1,0:T(1,128)} %all_to_all.87), calls=%async_computation.9 | async-start | bytes 3145728 | tf_op jit(solution)/shard_map/all_to_all | solution.py:112
  869.0 137.6 %all-gather.2.cloned.1.call-start = ((), (), s32[]{:S(2)}) async-start(), calls=%async_computation.10 | async-start | bytes 3145728 | tf_op jit(solution)/shard_map/all_gather | solution.py:126
  948.3 38.7 %slice-start = ((s8[6291456]{0:T(1024)(128)(4,1)}), s8[4194304]{0:T(1024)(128)(4,1)S(1)}, s32[]{:S(2)}) async-start(s8[6291456]{0:T(1024)(128)(4,1)} %bitcast.218), calls=%async_computation.11 | async-start | bytes 8388608
  948.3 38.7 %slice-start.2 = ((s8[8388608]{0:T(1024)(128)(4,1)}), s8[4194304]{0:T(1024)(128)(4,1)S(1)}, s32[]{:S(2)}) async-start(s8[8388608]{0:T(1024)(128)(4,1)} %bitcast.223), calls=%async_computation.13 | async-start | bytes 8388608
  966.9 20.1 %slice-start.1 = ((s8[6291456]{0:T(1024)(128)(4,1)}), s8[2097152]{0:T(1024)(128)(4,1)S(1)}, s32[]{:S(2)}) async-start(s8[6291456]{0:T(1024)(128)(4,1)} %bitcast.218), calls=%async_computation.12 | async-start | bytes 4194304
  966.9 20.1 %slice-start.3 = ((s8[8388608]{0:T(1024)(128)(4,1)}), s8[4194304]{0:T(1024)(128)(4,1)S(1)}, s32[]{:S(2)}) async-start(s8[8388608]{0:T(1024)(128)(4,1)} %bitcast.223), calls=%async_computation.14 | async-start | bytes 8388608
  987.0 19.6 %copy-start.6 = (f32[64,8192]{1,0:T(8,128)S(1)}, f32[64,8192]{1,0:T(8,128)}, u32[]{:S(2)}) copy-start(f32[64,8192]{1,0:T(8,128)} %reshape.357) | copy-start | bytes 6291460
  987.0 19.6 %copy-start.10 = (f32[64,64]{1,0:T(8,128)S(1)}, f32[64,64]{1,0:T(8,128)}, u32[]{:S(2)}) copy-start(f32[64,64]{1,0:T(8,128)} %param.16) | copy-start | bytes 49156
  (12 other events, 61.7 us)
Sparse Core Ops, SparseCore 0:
  904.5 33.4 all-gather.1
where the time goes:
time: 1040 us; the launch traced here: 1030 us
  local copies, waits for them, and re-layouts  411 us (40%)
  matrix products  343 us (33%)
  other arithmetic  77.7 us (7%)
  starting transfers between devices  65.4 us (6%)
  blocking collectives  61.9 us (6%)
  waiting for transfers between devices  55 us (5%)
  between operations  14.2 us (1%)
    dot_general x4, matrix products, body(): jnp.einsum('wlcma,mwaj->lmcj', shaped, basis_blocks, precision=highest)  76.9 us
    dot_general x4, matrix products, body(): jnp.einsum('lao,owmc->wlcma', updated[field_index], forward_tab, precisio...  72.3 us
    dot_general x4, matrix products, body(): jnp.einsum('wlcma,wmco->lao', shaped, inverse_tab, precision=highest)  71.8 us
    reshape x8, local copies, waits for them, and re-layouts, body(): exchanged.reshape(wave_count, lev_dev, complex_parts, m_dev, lat_dev)  70.1 us
    all_to_all x1, blocking collectives, body(): lax.all_to_all(slab, 'level', split_axis=2, concat_axis=1, tiled=True)  61.9 us
    unnamed x54, local copies, waits for them, and re-layouts  53.2 us
    all_to_all x1, waiting for transfers between devices, body(): lax.all_to_all(tendency, 'level', split_axis=1, concat_axis=2, tiled=True)  49.7 us
    transpose x4, local copies, waits for them, and re-layouts, body(): jnp.einsum('lao,owmc->wlcma', updated[field_index], forward_tab, precisio...  42.1 us
  transfers between devices with their start and end apart: 10, of which 4 were waited for; matrix products, arithmetic and copies ran while one was open for 39% of the time, Pallas kernels for 0%

commit v1 on v0

--- a/solution.py
+++ b/solution.py
@@ -87,7 +87,10 @@
     grid_field = jnp.stack(pieces)
     grid_low = grid_field.astype(jnp.bfloat16)
     slab = grid_low.reshape(fields, lev_dev, lat_dev * LON)
-    columns = lax.all_to_all(slab, "level", split_axis=2, concat_axis=1, tiled=True)
+    count = lax.axis_size("level")
+    blocks = jnp.stack(jnp.split(slab, count, axis=2), axis=0)
+    blocks = lax.all_to_all(blocks, "level", split_axis=0, concat_axis=0)
+    columns = jnp.concatenate(blocks, axis=1)
     col_count = columns.shape[2]
     tendency = column_physics(
         columns.reshape(fields * levels, col_count),

time: 1040 us -> 916 us (0.88)
  local copies, waits for them, and re-layouts: 411 us -> 306 us
    unnamed x54 -> x59, local copies, waits for them, and re-layouts: 53.2 us -> 10.9 us
    convert_element_type x2 -> x0, local copies, waits for them, and re-layouts: 22.8 us -> none  [column_physics(): values = columns.astype(jnp.float32)]
    all_to_all x1 -> x0, local copies, waits for them, and re-layouts: 22.8 us -> none  [body(): lax.all_to_all(slab, 'level', split_axis=2, concat_axis=1, tiled=True)]
    another operation x5, local copies, waits for them, and re-layouts: 32.1 us -> 11.6 us  [body(): grid_field = jnp.stack(pieces)]
  transfers between devices with their start and end apart: 10 -> 10, of which waited for: 4 -> 3; matrix products, arithmetic and copies ran while one was open for 39% -> 45% of each run, Pallas kernels for 0% -> 0%
where the time goes in v1:
time: 916 us; the launch traced here: 906 us
  matrix products  342 us (37%)
  local copies, waits for them, and re-layouts  306 us (33%)
  other arithmetic  69.2 us (8%)
  starting transfers between devices  62.2 us (7%)
  blocking collectives  56.6 us (6%)
  waiting for transfers between devices  55.1 us (6%)
  between operations  14.4 us (2%)
    dot_general x4, matrix products, body(): jnp.einsum('wlcma,mwaj->lmcj', shaped, basis_blocks, precision=highest)  76.7 us
    dot_general x4, matrix products, body(): jnp.einsum('lao,owmc->wlcma', updated[field_index], forward_tab, precisio...  72.4 us
    dot_general x4, matrix products, body(): jnp.einsum('wlcma,wmco->lao', shaped, inverse_tab, precision=highest)  71.4 us
    reshape x8, local copies, waits for them, and re-layouts, body(): exchanged.reshape(wave_count, lev_dev, complex_parts, m_dev, lat_dev)  70.8 us
    all_to_all x1, blocking collectives, body(): blocks = lax.all_to_all(blocks, 'level', split_axis=0, concat_axis=0)  56.6 us
    all_to_all x1, waiting for transfers between devices, body(): lax.all_to_all(tendency, 'level', split_axis=1, concat_axis=2, tiled=True)  49.8 us
    transpose x4, local copies, waits for them, and re-layouts, body(): jnp.einsum('lao,owmc->wlcma', updated[field_index], forward_tab, precisio...  42.3 us
    transpose x4, local copies, waits for them, and re-layouts, body(): jnp.einsum('lmcj,mwaj->wlcma', state[field_index], basis_blocks, precisio...  41.2 us
  transfers between devices with their start and end apart: 10, of which 3 were waited for; matrix products, arithmetic and copies ran while one was open for 45% of the time, Pallas kernels for 0%

profile of v1, /device:TPU:0, one launch (start us, length us, event | category | flops | bytes accessed | tf_op | source)
XLA Modules:
  0.0 905.7 jit_solution(2805521089622789569)
XLA Ops:
  24.3 10.3 %copy.55 = f32[16,32,2,16,24]{4,3,2,1,0:T(8,128)} copy(f32[16,32,2,16,24]{1,4,2,0,3:T(8,128)} %convolution_bitcast_fusion.8) | data formatting | bytes 3145728 | tf_op jit(solution)/shard_map/lmcj,mwaj->wlcma/transpose | solution.py:79
  133.5 12.3 %convolution_bitcast_fusion.5 = f32[16,32,2,16,24]{1,4,2,0,3:T(8,128)} fusion(f32[16,16,24,256,1]{3,2,4,1,0:T(8,128)} %bitcast.217, f32[1,32,16,2,256]{4,3,2,1,0:T(2,128)S(1)} %get-tuple-element.11), kind=kOutput, calls=%fused_computation.50 | convolution fusion | flops 1207959552 | bytes 8912896 | tf_op jit(solution)/shard_map/lmcj,mwaj->wlcma/dot_general | solution.py:79
  185.9 17.8 %bitcast_convert_fusion.3 = (bf16[32,24,768]{2,1,0:T(8,128)(2,1)}, f32[32,24,768,1,1]{2,1,3,0,4:T(8,128)}) fusion(f32[16,32,2,16,24]{4,3,2,1,0:T(8,128)} %reshape.344, f32[16,16,1,768]{3,1,2,0:T(8,128)} %get-tuple-element.18, f32[16,16,1,768]{3,1,2,0:T(8,128)S(1)} %get-tuple-element.17), kind=kOutput, calls=%fused_computation.67 | convolution fusion | flops 3624861696 | bytes 6684672 | tf_op jit(solution)/shard_map/wlcma,wmco->lao/dot_general | solution.py:86
  228.2 17.8 %bitcast_convert_fusion.2 = (bf16[32,24,768]{2,1,0:T(8,128)(2,1)}, f32[32,24,768,1,1]{2,1,3,0,4:T(8,128)}) fusion(f32[16,32,2,16,24]{4,3,2,1,0:T(8,128)} %reshape.345, f32[16,16,1,768]{3,1,2,0:T(8,128)} %get-tuple-element.18, f32[16,16,1,768]{3,1,2,0:T(8,128)S(1)} %get-tuple-element.17), kind=kOutput, calls=%fused_computation.66 | convolution fusion | flops 3624861696 | bytes 6684672 | tf_op jit(solution)/shard_map/wlcma,wmco->lao/dot_general | solution.py:86
  264.5 17.9 %bitcast_convert_fusion.1 = (bf16[32,24,768]{2,1,0:T(8,128)(2,1)}, f32[32,24,768,1,1]{2,1,3,0,4:T(8,128)}) fusion(f32[16,32,2,16,24]{4,3,2,1,0:T(8,128)} %reshape.346, f32[16,16,1,768]{3,1,2,0:T(8,128)} %get-tuple-element.18, f32[16,16,1,768]{3,1,2,0:T(8,128)S(1)} %get-tuple-element.17), kind=kOutput, calls=%fused_computation.65 | convolution fusion | flops 3624861696 | bytes 6684672 | tf_op jit(solution)/shard_map/wlcma,wmco->lao/dot_general | solution.py:86
  303.0 17.9 %bitcast_convert_fusion = (bf16[32,24,768]{2,1,0:T(8,128)(2,1)}, f32[32,24,768,1,1]{2,1,3,0,4:T(8,128)}) fusion(f32[16,32,2,16,24]{4,3,2,1,0:T(8,128)} %reshape.347, f32[16,16,1,768]{3,1,2,0:T(8,128)} %get-tuple-element.18, f32[16,16,1,768]{3,1,2,0:T(8,128)S(1)} %get-tuple-element.17), kind=kOutput, calls=%fused_computation.64 | convolution fusion | flops 3624861696 | bytes 6684672 | tf_op jit(solution)/shard_map/wlcma,wmco->lao/dot_general | solution.py:86
  331.6 56.6 %all_to_all.94 = bf16[2,4,32,9216]{3,2,1,0:T(8,128)(2,1)S(1)} all-to-all(bf16[2,4,32,9216]{3,2,1,0:T(8,128)(2,1)S(1)} %pad_maximum_fusion), channel_id=1, replica_groups=mesh['wave'=16,'level'=2] {'level'}, dimensions={0} | all-to-all | bytes 9437184 | tf_op jit(solution)/shard_map/all_to_all | solution.py:92
  391.8 18.9 %fusion.7.clone.4 = bf16[1024,9216]{0,1:T(8,128)(2,1)} fusion(bf16[256,9216]{1,0:T(8,128)(2,1)S(1)} %fusion.24, bf16[1024,256]{1,0:T(8,128)(2,1)S(1)} %copy-done.19, f32[1024]{0:T(1024)S(1)} %copy-done.21), kind=kOutput, calls=%fused_computation.9.clone.clone.clone.1 | convolution fusion | flops 4926210048 | bytes 24121344 | tf_op jit(solution)/shard_map/dot_general | solution.py:37
  410.7 38.9 %fusion.15 = bf16[1024,9216]{0,1:T(8,128)(2,1)} fusion(bf16[1024,1024]{1,0:T(8,128)(2,1)S(1)} %copy-done, f32[1024]{0:T(1024)S(1)} %copy-done.22, bf16[1024,9216]{0,1:T(8,128)(2,1)} %fusion.7.clone.4), kind=kOutput, calls=%fused_computation.17 | convolution fusion | flops 19421724672 | bytes 39849984 | tf_op jit(solution)/shard_map/dot_general | solution.py:40
  449.6 19.2 %fusion.21 = bf16[9216,256]{0,1:T(8,128)(2,1)S(1)} fusion(bf16[1024,9216]{0,1:T(8,128)(2,1)} %fusion.15, bf16[256,1024]{1,0:T(8,128)(2,1)S(1)} %copy-done.20, f32[256]{0:T(256)S(1)} %copy-done.23), kind=kOutput, calls=%fused_computation.24 | convolution fusion | flops 4836556800 | bytes 24118272 | tf_op jit(solution)/shard_map/dot_general | solution.py:43
  483.9 49.8 %all-to-all-done.5 = bf16[4,64,9216]{2,0,1:T(4,128)(2,1)} async-done(((bf16[4,64,9216]{2,0,1:T(4,128)(2,1)}), bf16[4,64,9216]{2,0,1:T(4,128)(2,1)}, u32[]{:S(2)}, u32[]{:S(2)}) %all-to-all-start.5) | async-done | bytes 4718624 | tf_op jit(solution)/shard_map/all_to_all | solution.py:106
  546.7 13.1 %reshape.355 = f32[4,32,24,768]{3,2,1,0:T(8,128)} reshape(f32[4,32,2,9216]{3,2,1,0:T(2,128)} %copy.69) | data formatting | bytes 18874368 | tf_op jit(solution)/shard_map/convert_element_type | solution.py:109
  570.1 17.0 %convolution_bitcast_fusion.3 = f32[16,32,2,16,24]{1,3,4,2,0:T(8,128)} fusion(f32[32,24,768,1,1]{2,1,0,4,3:T(8,128)S(1)} %get-tuple-element.8, f32[768,16,16,1]{0,2,3,1:T(8,128)S(1)} %get-tuple-element.16, f32[768,16,16,1]{0,2,3,1:T(8,128)S(1)} %get-tuple-element.15), kind=kOutput, calls=%fused_computation.48 | convolution fusion | flops 3624665088 | bytes 5505024 | tf_op jit(solution)/shard_map/lao,owmc->wlcma/dot_general | solution.py:112
  587.1 10.9 %copy.75 = f32[16,32,2,16,24]{4,3,2,1,0:T(8,128)} copy(f32[16,32,2,16,24]{1,3,4,2,0:T(8,128)} %convolution_bitcast_fusion.3) | data formatting | bytes 3145728 | tf_op jit(solution)/shard_map/lao,owmc->wlcma/transpose | solution.py:112
  612.5 18.5 %convolution_bitcast_fusion.4 = f32[16,32,2,16,24]{1,3,4,2,0:T(8,128)} fusion(f32[32,24,768,1,1]{2,1,0,4,3:T(8,128)} %get-tuple-element.5, f32[768,16,16,1]{0,2,3,1:T(8,128)} %copy-done.9, f32[768,16,16,1]{0,2,3,1:T(8,128)S(1)} %get-tuple-element.15), kind=kOutput, calls=%fused_computation.49 | convolution fusion | flops 3624665088 | bytes 5505024 | tf_op jit(solution)/shard_map/lao,owmc->wlcma/dot_general | solution.py:112
  630.9 10.5 %copy.71 = f32[16,32,2,16,24]{4,3,2,1,0:T(8,128)} copy(f32[16,32,2,16,24]{1,3,4,2,0:T(8,128)} %convolution_bitcast_fusion.4) | data formatting | bytes 3145728 | tf_op jit(solution)/shard_map/lao,owmc->wlcma/transpose | solution.py:112
  657.9 18.5 %convolution_bitcast_fusion.2 = f32[16,32,2,16,24]{1,3,4,2,0:T(8,128)} fusion(f32[32,24,768,1,1]{2,1,0,4,3:T(8,128)} %get-tuple-element.7, f32[768,16,16,1]{0,2,3,1:T(8,128)} %copy-done.9, f32[768,16,16,1]{0,2,3,1:T(8,128)S(1)} %get-tuple-element.15), kind=kOutput, calls=%fused_computation.47 | convolution fusion | flops 3624665088 | bytes 5505024 | tf_op jit(solution)/shard_map/lao,owmc->wlcma/dot_general | solution.py:112
  676.3 10.5 %copy.80 = f32[16,32,2,16,24]{4,3,2,1,0:T(8,128)} copy(f32[16,32,2,16,24]{1,3,4,2,0:T(8,128)} %convolution_bitcast_fusion.2) | data formatting | bytes 3145728 | tf_op jit(solution)/shard_map/lao,owmc->wlcma/transpose | solution.py:112
  702.3 18.5 %convolution_bitcast_fusion.1 = f32[16,32,2,16,24]{1,3,4,2,0:T(8,128)} fusion(f32[32,24,768,1,1]{2,1,0,4,3:T(8,128)} %get-tuple-element.6, f32[768,16,16,1]{0,2,3,1:T(8,128)} %copy-done.9, f32[768,16,16,1]{0,2,3,1:T(8,128)S(1)} %get-tuple-element.15), kind=kOutput, calls=%fused_computation.46 | convolution fusion | flops 3624665088 | bytes 5505024 | tf_op jit(solution)/shard_map/lao,owmc->wlcma/dot_general | solution.py:112
  720.8 10.5 %copy.84 = f32[16,32,2,16,24]{4,3,2,1,0:T(8,128)} copy(f32[16,32,2,16,24]{1,3,4,2,0:T(8,128)} %convolution_bitcast_fusion.1) | data formatting | bytes 3145728 | tf_op jit(solution)/shard_map/lao,owmc->wlcma/transpose | solution.py:112
  760.7 18.7 %fusion.42 = f32[32,16,2,256]{3,0,2,1:T(8,128)S(1)} fusion(f32[16,16,24,256,1]{3,2,1,4,0:T(8,128)} %bitcast.218, f32[16,32,2,16,24]{4,3,2,1,0:T(8,128)} %reshape.350), kind=kOutput, calls=%fused_computation.72 | convolution fusion | flops 1207959552 | bytes 8912896 | tf_op jit(solution)/shard_map/wlcma,mwaj->lmcj/dot_general | solution.py:119
  826.0 18.6 %fusion.39 = f32[1,32,16,2,256]{4,1,3,2,0:T(8,128)S(1)} fusion(f32[16,16,24,256,1]{3,2,1,4,0:T(8,128)} %bitcast.219, f32[16,32,2,16,24]{4,3,2,1,0:T(8,128)} %reshape.349), kind=kOutput, calls=%fused_computation.71 | convolution fusion | flops 1207959552 | bytes 8912896 | tf_op jit(solution)/shard_map/wlcma,mwaj->lmcj/dot_general | solution.py:119
  844.7 19.8 %fusion.45 = f32[1,32,16,2,256]{4,1,3,2,0:T(8,128)} fusion(f32[16,16,24,256,1]{3,2,1,4,0:T(8,128)} %bitcast.220, f32[16,32,2,16,24]{4,3,2,1,0:T(8,128)} %reshape.352), kind=kOutput, calls=%fused_computation.73 | convolution fusion | flops 1207959552 | bytes 8912896 | tf_op jit(solution)/shard_map/wlcma,mwaj->lmcj/dot_general | solution.py:119
  864.6 19.7 %fusion.48 = f32[1,32,16,2,256]{4,1,3,2,0:T(8,128)} fusion(f32[16,16,24,256,1]{3,2,1,4,0:T(8,128)S(1)} %bitcast.223, f32[16,32,2,16,24]{4,3,2,1,0:T(8,128)S(1)} %bitcast.225), kind=kOutput, calls=%fused_computation.74 | convolution fusion | flops 1207959552 | bytes 8912896 | tf_op jit(solution)/shard_map/wlcma,mwaj->lmcj/dot_general | solution.py:119
  (150 shorter events, 409.2 us)
Async XLA Ops:
  6.5 404.2 %copy-start = (bf16[1024,1024]{1,0:T(8,128)(2,1)S(1)}, bf16[1024,1024]{1,0:T(8,128)(2,1)}, u32[]{:S(2)}) copy-start(bf16[1024,1024]{1,0:T(8,128)(2,1)} %param.22) | copy-start | bytes 6291460
  43.7 39.6 %all-to-all-start = ((f32[16,1,24576]{2,1,0:T(1,128)}), f32[16,1,24576]{2,1,0:T(1,128)}, u32[]{:S(2)}, u32[]{:S(2)}) async-start(f32[16,1,24576]{2,1,0:T(1,128)} %all_to_all.76), calls=%async_computation | async-start | bytes 3145728 | tf_op jit(solution)/shard_map/all_to_all | solution.py:82
  83.3 41.0 %all-to-all-start.1 = ((f32[16,1,24576]{2,1,0:T(1,128)}), f32[16,1,24576]{2,1,0:T(1,128)}, u32[]{:S(2)}, u32[]{:S(2)}) async-start(f32[16,1,24576]{2,1,0:T(1,128)} %all_to_all.77), calls=%async_computation.1 | async-start | bytes 3145728 | tf_op jit(solution)/shard_map/all_to_all | solution.py:82
  124.3 97.6 %all-to-all-start.2 = ((f32[16,1,24576]{2,1,0:T(1,128)}), f32[16,1,24576]{2,1,0:T(1,128)}, u32[]{:S(2)}, u32[]{:S(2)}) async-start(f32[16,1,24576]{2,1,0:T(1,128)} %all_to_all.78), calls=%async_computation.2 | async-start | bytes 3145728 | tf_op jit(solution)/shard_map/all_to_all | solution.py:82
  221.9 65.5 %all-to-all-start.3 = ((f32[16,1,24576]{2,1,0:T(1,128)}), f32[16,1,24576]{2,1,0:T(1,128)}, u32[]{:S(2)}, u32[]{:S(2)}) async-start(f32[16,1,24576]{2,1,0:T(1,128)} %all_to_all.79), calls=%async_computation.3 | async-start | bytes 3145728 | tf_op jit(solution)/shard_map/all_to_all | solution.py:82
  391.7 19.0 %copy-start.22 = (f32[1024]{0:T(1024)S(1)}, f32[1024]{0:T(1024)}, u32[]{:S(2)}) copy-start(f32[1024]{0:T(1024)} %param.23) | copy-start | bytes 12292
  410.7 38.9 %copy-start.20 = (bf16[256,1024]{1,0:T(8,128)(2,1)S(1)}, bf16[256,1024]{1,0:T(8,128)(2,1)}, u32[]{:S(2)}) copy-start(bf16[256,1024]{1,0:T(8,128)(2,1)} %param.24) | copy-start | bytes 1572868
  410.7 38.9 %copy-start.23 = (f32[256]{0:T(256)S(1)}, f32[256]{0:T(256)}, u32[]{:S(2)}) copy-start(f32[256]{0:T(256)} %param.25) | copy-start | bytes 3076
  474.7 59.0 %all-to-all-start.5 = ((bf16[4,64,9216]{2,0,1:T(4,128)(2,1)}), bf16[4,64,9216]{2,0,1:T(4,128)(2,1)}, u32[]{:S(2)}, u32[]{:S(2)}) async-start(bf16[4,64,9216]{2,0,1:T(4,128)(2,1)} %copy.67), calls=%async_computation.5 | async-start | bytes 9437184 | tf_op jit(solution)/shard_map/all_to_all | solution.py:106
  483.9 86.2 %copy-start.9 = (f32[768,16,16,1]{0,2,3,1:T(8,128)}, f32[768,16,16,1]{0,2,3,1:T(8,128)S(1)}, u32[]{:S(2)}) copy-start(f32[768,16,16,1]{0,2,3,1:T(8,128)S(1)} %get-tuple-element.16) | copy-start | bytes 2359300
  607.1 43.4 %all-to-all-start.7 = ((f32[16,1,24576]{2,1,0:T(1,128)}), f32[16,1,24576]{2,1,0:T(1,128)S(1)}, u32[]{:S(2)}, u32[]{:S(2)}) async-start(f32[16,1,24576]{2,1,0:T(1,128)} %all_to_all.81), calls=%async_computation.7 | async-start | bytes 3145728 | tf_op jit(solution)/shard_map/all_to_all | solution.py:115
  651.7 44.3 %all-to-all-start.6 = ((f32[16,1,24576]{2,1,0:T(1,128)}), f32[16,1,24576]{2,1,0:T(1,128)S(1)}, u32[]{:S(2)}, u32[]{:S(2)}) async-start(f32[16,1,24576]{2,1,0:T(1,128)} %all_to_all.80), calls=%async_computation.6 | async-start | bytes 3145728 | tf_op jit(solution)/shard_map/all_to_all | solution.py:115
  696.0 24.8 %copy-start.4 = (f32[16,1,24576]{2,1,0:T(1,128)}, f32[16,1,24576]{2,1,0:T(1,128)S(1)}, u32[]{:S(2)}) copy-start(f32[16,1,24576]{2,1,0:T(1,128)S(1)} %all-to-all-done.6) | copy-start | bytes 4718596
  696.0 44.5 %all-to-all-start.8 = ((f32[16,1,24576]{2,1,0:T(1,128)}), f32[16,1,24576]{2,1,0:T(1,128)}, u32[]{:S(2)}, u32[]{:S(2)}) async-start(f32[16,1,24576]{2,1,0:T(1,128)} %all_to_all.82), calls=%async_computation.8 | async-start | bytes 3145728 | tf_op jit(solution)/shard_map/all_to_all | solution.py:115
  731.3 15.4 %copy-start.14 = (s32[16]{0:T(128)S(1)}, s32[16]{0:T(128)}, u32[]{:S(2)}) copy-start(s32[16]{0:T(128)} %copy-done.13) | copy-start | bytes 196
  731.3 15.5 %copy-start.16 = (f32[64]{0:T(128)S(1)}, f32[64]{0:T(128)}, u32[]{:S(2)}) copy-start(f32[64]{0:T(128)} %param.17) | copy-start | bytes 772
  740.4 71.9 %all-to-all-start.9 = ((f32[16,1,24576]{2,1,0:T(1,128)}), f32[16,1,24576]{2,1,0:T(1,128)}, u32[]{:S(2)}, u32[]{:S(2)}) async-start(f32[16,1,24576]{2,1,0:T(1,128)} %all_to_all.83), calls=%async_computation.9 | async-start | bytes 3145728 | tf_op jit(solution)/shard_map/all_to_all | solution.py:115
  746.6 137.6 %all-gather.2.cloned.1.call-start = ((), (), s32[]{:S(2)}) async-start(), calls=%async_computation.10 | async-start | bytes 3145728 | tf_op jit(solution)/shard_map/all_gather | solution.py:129
  826.0 38.4 %slice-start = ((s8[6291456]{0:T(1024)(128)(4,1)}), s8[4194304]{0:T(1024)(128)(4,1)S(1)}, s32[]{:S(2)}) async-start(s8[6291456]{0:T(1024)(128)(4,1)} %bitcast.221), calls=%async_computation.11 | async-start | bytes 8388608
  826.0 38.5 %slice-start.2 = ((s8[8388608]{0:T(1024)(128)(4,1)}), s8[4194304]{0:T(1024)(128)(4,1)S(1)}, s32[]{:S(2)}) async-start(s8[8388608]{0:T(1024)(128)(4,1)} %bitcast.224), calls=%async_computation.13 | async-start | bytes 8388608
  844.7 19.8 %slice-start.1 = ((s8[6291456]{0:T(1024)(128)(4,1)}), s8[2097152]{0:T(1024)(128)(4,1)S(1)}, s32[]{:S(2)}) async-start(s8[6291456]{0:T(1024)(128)(4,1)} %bitcast.221), calls=%async_computation.12 | async-start | bytes 4194304
  844.7 19.8 %slice-start.3 = ((s8[8388608]{0:T(1024)(128)(4,1)}), s8[4194304]{0:T(1024)(128)(4,1)S(1)}, s32[]{:S(2)}) async-start(s8[8388608]{0:T(1024)(128)(4,1)} %bitcast.224), calls=%async_computation.14 | async-start | bytes 8388608
  864.5 19.7 %copy-start.8 = (f32[64,8192]{1,0:T(8,128)S(1)}, f32[64,8192]{1,0:T(8,128)}, u32[]{:S(2)}) copy-start(f32[64,8192]{1,0:T(8,128)} %reshape.351) | copy-start | bytes 6291460
  864.6 19.7 %copy-start.12 = (f32[64,64]{1,0:T(8,128)S(1)}, f32[64,64]{1,0:T(8,128)}, u32[]{:S(2)}) copy-start(f32[64,64]{1,0:T(8,128)} %param.16) | copy-start | bytes 49156
  (14 other events, 54.1 us)
Sparse Core Ops, SparseCore 0:
  782.2 33.4 all-gather.1
